TPU v7x, 256 devices: a whole 4x4x8 slice. The times are simulated.
256 devices in a mesh: lon: 32 (over z, y_hi, core), lat: 8 (over y_lo, x).
Axes of the slice: x: 4, y: 4 (y_hi: 2, y_lo: 2; y = y_hi * 2 + y_lo), z: 8, core: 2. Of those that a mesh axis runs over, the one named last changes fastest.
Arguments:
- state: bfloat16 [360, 768, 128], P('lat', 'lon'), may hold values from -6 to 6
- land_sea: int32 [360, 768], P('lat', 'lon'), may hold values 0 or 1
- cotangent: bfloat16 [360, 768, 128], P('lat', 'lon'), may hold values from -6 to 6
- dw_kernel: bfloat16 [2, 7, 7, 128], replicated, may hold values from -0.875 to 0.875
- conv_bias: float32 [2, 128], replicated, may hold values from -3 to 3
- norm_gain: float32 [2, 128], replicated, may hold values from 0.1 to 1.9
- norm_bias: float32 [2, 128], replicated, may hold values from -3 to 3
- weight_in: bfloat16 [2, 128, 512], replicated, may hold values from -0.5 to 0.5
- bias_in: float32 [2, 512], replicated, may hold values from -3 to 3
- weight_out: bfloat16 [2, 512, 128], replicated, may hold values from -0.25 to 0.25
- bias_out: float32 [2, 128], replicated, may hold values from -3 to 3
- layer_scale: float32 [2, 128], replicated, may hold values from 0.3 to 1
Outputs:
- output: bfloat16 [360, 768, 128], P('lat', 'lon')
- grad_state: bfloat16 [360, 768, 128], P('lat', 'lon')
- grad_dw_kernel: float32 [2, 7, 7, 128], replicated
- grad_conv_bias: float32 [2, 128], replicated
- grad_norm_gain: float32 [2, 128], replicated
- grad_norm_bias: float32 [2, 128], replicated
- grad_weight_in: float32 [2, 128, 512], replicated
- grad_bias_in: float32 [2, 512], replicated
- grad_weight_out: float32 [2, 512, 128], replicated
- grad_bias_out: float32 [2, 128], replicated
- grad_layer_scale: float32 [2, 128], replicated
All inputs are finite; a program needn't handle non-finite values. No bound on the sum of `land_sea` on one device may be relied on, other than what follows from the above.
Results may differ from a plain program's by a relative error of at most 0.02.
Values may be sent and summed in bfloat16 or wider, within the bound.
A program may use at most 64 MiB of HBM per device.

v0:
```python
import math
import jax
import jax.numpy as jnp
from jax import lax
from jax.sharding import PartitionSpec as P

KSIZE = 7
BLOCKS = 2
EPS_NORM = 1e-06
INV_ROOT_TWO = 0.7071067811865476
INV_ROOT_TWO_PI = 0.3989422804014327


def with_halo(shard, sides, width, wrap):
    for axis, dim in sides:
        count, length = (lax.axis_size(axis), shard.shape[dim])
        up = [(i, (i + 1) % count) for i in range(count if wrap else count - 1)]
        down = [(j, i) for i, j in up]
        last = lax.slice_in_dim(shard, length - width, length, axis=dim)
        first = lax.slice_in_dim(shard, 0, width, axis=dim)
        before = lax.ppermute(last, axis, up)
        after = lax.ppermute(first, axis, down)
        shard = jnp.concatenate([before, shard, after], axis=dim)
    return shard


def depthwise(window, kernel, height, breadth):
    summed = jnp.zeros((height, breadth, window.shape[2]), jnp.float32)
    for tap_row in range(KSIZE):
        for tap_col in range(KSIZE):
            piece = window[tap_row : tap_row + height, tap_col : tap_col + breadth].astype(
                jnp.float32
            )
            summed = summed + piece * kernel[tap_row, tap_col].astype(jnp.float32)
    return summed


def block_forward(window, land_rows, params):
    (
        kernel,
        conv_bias,
        norm_gain,
        norm_bias,
        weight_in,
        bias_in,
        weight_out,
        bias_out,
        layer_scale,
    ) = params
    margin = KSIZE // 2
    height = window.shape[0] - 2 * margin
    breadth = window.shape[1] - 2 * margin
    channels = window.shape[2]
    cell_count = height * breadth
    mixed_sum = depthwise(window, kernel, height, breadth) + conv_bias
    center = mixed_sum - jnp.mean(mixed_sum, axis=-1, keepdims=True)
    inverse = lax.rsqrt(jnp.mean(center * center, axis=-1, keepdims=True) + EPS_NORM)
    normed = (center * inverse).reshape(cell_count, channels)
    lifted = (normed * norm_gain + norm_bias).astype(jnp.bfloat16)
    hidden = jnp.dot(lifted, weight_in, preferred_element_type=jnp.float32) + bias_in
    active = jax.nn.gelu(hidden, approximate=False).astype(jnp.bfloat16)
    branch = jnp.dot(active, weight_out, preferred_element_type=jnp.float32) + bias_out
    interior = (
        window[margin : margin + height, margin : margin + breadth]
        .astype(jnp.float32)
        .reshape(cell_count, channels)
    )
    ocean_mask = land_rows.reshape(cell_count, 1).astype(jnp.float32)
    result = (
        ((interior + layer_scale * branch) * ocean_mask)
        .astype(jnp.bfloat16)
        .reshape(height, breadth, channels)
    )
    return (result, (normed, inverse.reshape(cell_count, 1), lifted, hidden, active, branch))


def block_backward(window, land_rows, incoming, params, stored):
    (
        kernel,
        conv_bias,
        norm_gain,
        norm_bias,
        weight_in,
        bias_in,
        weight_out,
        bias_out,
        layer_scale,
    ) = params
    normed, inverse, lifted, hidden, active, branch = stored
    margin = KSIZE // 2
    height = window.shape[0] - 2 * margin
    breadth = window.shape[1] - 2 * margin
    channels = window.shape[2]
    cell_count = height * breadth
    ocean_mask = land_rows.reshape(cell_count, 1).astype(jnp.float32)
    masked = incoming.reshape(cell_count, channels).astype(jnp.float32) * ocean_mask
    grad_branch = (masked * layer_scale).astype(jnp.bfloat16)
    contract_rows = (((0,), (0,)), ((), ()))
    contract_cols = (((1,), (1,)), ((), ()))
    grad_scale = jnp.sum(masked * branch, axis=0)
    grad_bias_out = jnp.sum(grad_branch.astype(jnp.float32), axis=0)
    grad_weight_out = lax.dot_general(
        active, grad_branch, contract_rows, preferred_element_type=jnp.float32
    )
    grad_active = lax.dot_general(
        grad_branch, weight_out, contract_cols, preferred_element_type=jnp.float32
    )
    cumulative = 0.5 * (1.0 + lax.erf(hidden * INV_ROOT_TWO))
    density = jnp.exp(-0.5 * hidden * hidden) * INV_ROOT_TWO_PI
    grad_hidden = (grad_active * (cumulative + hidden * density)).astype(jnp.bfloat16)
    grad_bias_in = jnp.sum(grad_hidden.astype(jnp.float32), axis=0)
    grad_weight_in = lax.dot_general(
        lifted, grad_hidden, contract_rows, preferred_element_type=jnp.float32
    )
    grad_lifted = lax.dot_general(
        grad_hidden, weight_in, contract_cols, preferred_element_type=jnp.float32
    )
    grad_gain = jnp.sum(grad_lifted * normed, axis=0)
    grad_shift = jnp.sum(grad_lifted, axis=0)
    scaled = grad_lifted * norm_gain
    grad_mixed = inverse * (
        scaled
        - jnp.mean(scaled, axis=-1, keepdims=True)
        - normed * jnp.mean(scaled * normed, axis=-1, keepdims=True)
    )
    grad_mixed = grad_mixed.astype(jnp.bfloat16).reshape(height, breadth, channels)
    spread = grad_mixed.astype(jnp.float32)
    grad_conv_bias = jnp.sum(spread, axis=(0, 1))
    tap_sums = []
    for tap_row in range(KSIZE):
        for tap_col in range(KSIZE):
            piece = window[tap_row : tap_row + height, tap_col : tap_col + breadth].astype(
                jnp.float32
            )
            tap_sums.append(jnp.sum(spread * piece, axis=(0, 1)))
    grad_kernel = jnp.stack(tap_sums).reshape(KSIZE, KSIZE, channels)
    gradients = (
        grad_kernel,
        grad_conv_bias,
        grad_gain,
        grad_shift,
        grad_weight_in,
        grad_bias_in,
        grad_weight_out,
        grad_bias_out,
        grad_scale,
    )
    return (grad_mixed, masked.reshape(height, breadth, channels), gradients)


def adjoint(padded, masked, kernel):
    margin = KSIZE // 2
    height = masked.shape[0]
    breadth = masked.shape[1]
    summed = masked
    for tap_row in range(KSIZE):
        for tap_col in range(KSIZE):
            first_row = 2 * margin - tap_row
            first_col = 2 * margin - tap_col
            piece = padded[first_row : first_row + height, first_col : first_col + breadth].astype(
                jnp.float32
            )
            summed = summed + piece * kernel[tap_row, tap_col].astype(jnp.float32)
    return summed.astype(jnp.bfloat16)


def extend(tile_field):
    beside_all = with_halo(tile_field, (("lon", 1),), KSIZE // 2, True)
    return with_halo(beside_all, (("lat", 0),), KSIZE // 2, False)


def sum_everything(parts):
    (
        kernel_part,
        conv_part,
        gain_part,
        shift_part,
        first_part,
        first_bias,
        second_part,
        second_bias,
        scale_part,
    ) = parts
    return lax.psum(
        (
            kernel_part,
            conv_part,
            gain_part,
            shift_part,
            first_part,
            first_bias,
            second_part,
            second_bias,
            scale_part,
        ),
        ("lon", "lat"),
    )


def on_device(
    state,
    land_sea,
    cotangent,
    dw_kernel,
    conv_bias,
    norm_gain,
    norm_bias,
    weight_in,
    bias_in,
    weight_out,
    bias_out,
    layer_scale,
):
    stacked = (
        dw_kernel,
        conv_bias,
        norm_gain,
        norm_bias,
        weight_in,
        bias_in,
        weight_out,
        bias_out,
        layer_scale,
    )
    height = state.shape[0]
    breadth = state.shape[1]
    grad_norm = 1.0 / math.sqrt(lax.axis_size("lat") * height * lax.axis_size("lon") * breadth)
    current = state
    windows = []
    stored_all = []
    for layer_index in range(BLOCKS):
        params = tuple((member[layer_index] for member in stacked))
        window = extend(current)
        windows.append(window)
        outcome = block_forward(window, land_sea, params)
        current = outcome[0]
        stored_all.append(outcome[1])
    incoming = cotangent
    per_layer = [None] * BLOCKS
    for layer_index in reversed(range(BLOCKS)):
        params = tuple((member[layer_index] for member in stacked))
        stored = stored_all[layer_index]
        grad_mixed, masked, gradients = block_backward(
            windows[layer_index], land_sea, incoming, params, stored
        )
        incoming = adjoint(extend(grad_mixed), masked, params[0])
        per_layer[layer_index] = gradients
    combined = tuple(
        (
            jnp.stack([per_layer[layer_index][member] for layer_index in range(BLOCKS)])
            for member in range(9)
        )
    )
    combined = sum_everything(combined)
    scaled = [member * grad_norm for member in combined]
    return (
        current,
        incoming,
        scaled[0],
        scaled[1],
        scaled[2],
        scaled[3],
        scaled[4],
        scaled[5],
        scaled[6],
        scaled[7],
        scaled[8],
    )


def solution(mesh):
    placed = (
        P("lat", "lon", None),
        P("lat", "lon"),
        P("lat", "lon", None),
        P(),
        P(),
        P(),
        P(),
        P(),
        P(),
        P(),
        P(),
        P(),
    )
    return jax.shard_map(
        on_device,
        mesh=mesh,
        in_specs=placed,
        out_specs=(
            P("lat", "lon", None),
            P("lat", "lon", None),
            P(),
            P(),
            P(),
            P(),
            P(),
            P(),
            P(),
            P(),
            P(),
        ),
        check_vma=False,
    )
```

profile of v0, /device:TPU:2, one launch (start us, length us, event | category | flops | bytes accessed | tf_op | source)
XLA Modules:
  0.0 509.7 jit_solution(3118116453118885206)
XLA Ops:
  7.2 1.0 fusion.426
  8.3 8.0 %collective-permute-start.1 = (bf16[45,3,128]{2,1,0:T(4,128)(2,1)S(1)}, bf16[45,3,128]{2,1,0:T(4,128)(2,1)S(1)}, u32[]{:S(2)}, u32[]{:S(2)}) collective-permute-start(bf16[45,3,128]{2,1,0:T(4,128)(2,1)S(1)} %get-tuple-element.208), channel_id=1, source_target_pairs={{8,0},{16,8},{24,16},{32,24},{40,32},{48,40},{56,48},{64,56},{72,6... | collective-permute-start | bytes 103688 | tf_op jit(solution)/shard_map/ppermute | solution.py:22
  16.3 0.9 fusion.427
  17.6 0.6 fusion.415
  18.2 1.3 slice_bitcast_fusion.101
  19.5 1.3 fusion.428
  20.9 0.7 convert_element_type.1162
  21.7 0.7 fusion.365
  22.3 1.3 slice_bitcast_fusion.99
  23.6 1.3 slice_bitcast_fusion.98
  24.9 2.5 convert_reduce_fusion.3
  27.3 1.0 constant_dynamic-update-slice_fusion.1
  28.4 0.8 pad_maximum_fusion.25
  29.2 3.4 collective-permute-start.2
  32.6 2.4 collective-permute-start.3
  35.1 3.2 collective-permute-done.3
  38.6 5.0 fusion.421
  44.7 6.0 %fusion.4 = (bf16[1080,512]{1,0:T(8,128)(2,1)S(1)}, f32[1080,512]{1,0:T(8,128)}) fusion(f32[512]{0:T(512)S(1)} %bitcast.782, bf16[1080,128]{1,0:T(8,128)(2,1)S(1)} %bitcast.742, bf16[2,128,512]{2,1,0:T(8,128)(2,1)S(1)} %copy-done.11), kind=kOutput, calls=%fused_computation.113 | convolution fusion | flops 178053120 | bytes 3727360 | tf_op jit(solution)/shard_map/dot_general | solution.py:60
  50.8 1.0 copy-done.2
  51.8 1.3 fusion.277
  53.2 5.3 %collective-permute-start.5 = (bf16[45,3,128]{2,1,0:T(4,128)(2,1)S(1)}, bf16[45,3,128]{2,1,0:T(4,128)(2,1)S(1)}, u32[]{:S(2)}, u32[]{:S(2)}) collective-permute-start(bf16[45,3,128]{2,1,0:T(4,128)(2,1)S(1)} %get-tuple-element.206), channel_id=1, source_target_pairs={{8,0},{16,8},{24,16},{32,24},{40,32},{48,40},{56,48},{64,56},{72,6... | collective-permute-start | bytes 103688 | tf_op jit(solution)/shard_map/ppermute | solution.py:22
  58.8 1.5 collective-permute-done.4
  60.3 3.1 collective-permute-start.6
  63.4 3.1 collective-permute-start.7
  66.8 3.1 collective-permute-done.7
  70.1 5.0 fusion.419
  75.4 0.8 copy-done.1
  77.2 1.5 add_convert_fusion.2
  78.7 7.0 %fusion.7 = (bf16[1080,512]{1,0:T(8,128)(2,1)}, f32[1080,512]{1,0:T(8,128)S(1)}) fusion(f32[512]{0:T(512)} %bitcast.780, bf16[1080,128]{1,0:T(8,128)(2,1)S(1)} %bitcast.741, bf16[2,128,512]{2,1,0:T(8,128)(2,1)} %param.19), kind=kOutput, calls=%fused_computation.116 | convolution fusion | flops 178053120 | bytes 3727360 | tf_op jit(solution)/shard_map/dot_general | solution.py:60
  85.7 1.9 convert_reduce_fusion
  87.6 1.1 fusion.417
  88.7 1.0 convert_reduce_fusion.2
  89.7 1.6 fusion.201
  91.3 1.6 fusion.174
  93.1 5.3 %collective-permute-start.9 = (bf16[45,3,128]{2,1,0:T(4,128)(2,1)S(1)}, bf16[45,3,128]{2,1,0:T(4,128)(2,1)S(1)}, u32[]{:S(2)}, u32[]{:S(2)}) collective-permute-start(bf16[45,3,128]{2,1,0:T(4,128)(2,1)S(1)} %get-tuple-element.204), channel_id=1, source_target_pairs={{8,0},{16,8},{24,16},{32,24},{40,32},{48,40},{56,48},{64,56},{72,6... | collective-permute-start | bytes 103688 | tf_op jit(solution)/shard_map/ppermute | solution.py:22
  98.4 1.7 fusion.200
  100.4 2.2 collective-permute-start.10
  102.6 12.7 %collective-permute-start.11 = (bf16[3,30,128]{2,1,0:T(8,128)(2,1)S(1)}, bf16[3,30,128]{2,1,0:T(8,128)(2,1)S(1)}, u32[]{:S(2)}, u32[]{:S(2)}) collective-permute-start(bf16[3,30,128]{2,1,0:T(8,128)(2,1)S(1)} %get-tuple-element.191), channel_id=1, source_target_pairs={{0,1},{1,2},{2,3},{3,4},{4,5},{5,6},{6,7},{8,9},{9,10},{10,11},{11... | collective-permute-start | bytes 69128 | tf_op jit(solution)/shard_map/ppermute | solution.py:21
  115.8 4.9 stack.474
  120.7 1.1 pad_maximum_fusion.4
  122.0 6.2 %multiply_convert_fusion.1 = (bf16[1080,128]{1,0:T(8,128)(2,1)S(1)}, bf16[45,24,128]{2,1,0:T(8,128)(2,1)S(1)}) fusion(f32[1080]{0:T(1024)S(1)} %convert_element_type.1163, f32[128]{0:T(128)S(1)} %copy-done.21, f32[128]{0:T(128)S(1)} %copy-done.102, bf16[48,30,128]{2,1,0:T(8,128)(2,1)S(1)} %get-tuple-element.189, f32[128]{0:T(128)S(1)} %copy-done.104, ...), kind=kLoop, calls=%fused_computation.516 | loop fusion | flops 23777280 | bytes 12821440 | tf_op jit(solution)/shard_map/convert_element_type | solution.py:97
  128.5 1.9 convert_reduce_fusion.1
  130.4 1.1 convolution_bitcast_fusion.3
  131.4 1.1 fusion.416
  133.0 1.6 fusion.247
  134.6 1.6 fusion.275
  136.3 0.7 fusion.423
  137.5 2.4 multiply_reduce_fusion.1
  140.8 1.1 fusion.274
  142.2 0.8 stack.424
  143.0 0.7 pad_maximum_fusion.31
  143.8 81.3 %all-reduce = (f32[2,7,7,128]{3,2,1,0:T(8,128)S(1)}, f32[2,128]{1,0:T(2,128)S(1)}, f32[2,128]{1,0:T(2,128)S(1)}, f32[2,128]{1,0:T(2,128)S(1)}, f32[2,512]{1,0:T(...) all-reduce(f32[2,7,7,128]{3,2,1,0:T(8,128)S(1)} %pad_maximum_fusion, ...), channel_id=1, replica_groups=mesh['lon'=32,'lat'=8] {'lon','lat'}, use_global_device_ids=true, to_apply=%region_106.0 | all-reduce | flops 14848 | bytes 118784 | tf_op jit(solution)/shard_map/psum | solution.py:184
  228.0 0.6 broadcast_multiply_fusion.9
  229.7 0.8 pad_maximum_fusion.1
  230.7 6.0 %collective-permute-done.12 = bf16[45,3,128]{2,1,0:T(4,128)(2,1)S(1)} collective-permute-done((bf16[45,3,128]{2,1,0:T(4,128)(2,1)S(1)}, bf16[45,3,128]{2,1,0:T(4,128)(2,1)S(1)}, u32[]{:S(2)}, u32[]{:S(2)}) %collective-permute-start.12) | collective-permute-done | bytes 34592 | tf_op jit(solution)/shard_map/ppermute | solution.py:21
  236.7 2.6 collective-permute-start.14
  239.3 3.2 collective-permute-start.15
  242.6 0.8 pad_maximum_fusion
  243.4 0.6 copy.30
  244.1 1.0 collective-permute-done.15
  245.6 5.8 %fusion.280 = bf16[45,24,128]{2,1,0:T(8,128)(2,1)} fusion(bf16[45,24,128]{2,1,0:T(8,128)(2,1)S(1)} %bitcast.724, bf16[45,24,128]{2,1,0:T(8,128)(2,1)S(1)} %get-tuple-element.167, bf16[45,3,128]{2,1,0:T(4,128)(2,1)S(1)} %collective-permute-done.12, bf16[45,3,128]{2,1,0:T(4,128)(2,1)S(1)} %collective-permute-done.13, ...), kind=kLoop, calls=%fused_computation.534 | loop fusion | flops 23224320 | bytes 12540128 | tf_op jit(solution)/shard_map/convert_element_type | solution.py:164
  251.4 247.4 %all-reduce.4.cloned.1.call-done = (f32[2,128,512]{2,1,0:T(8,128)}, f32[2,512,128]{2,1,0:T(8,128)}) async-done(((f32[2,128,512]{2,1,0:T(8,128)}, f32[2,512,128]{2,1,0:T(8,128)}), (f32[2,128,512]{2,1,0:T(8,128)}, f32[2,512,128]{2,1,0:T(8,128)})) %all-reduce.4.cloned.1.call-update) | async-done | bytes 1048592 | tf_op jit(solution)/shard_map/psum | solution.py:184
  498.8 1.9 broadcast_multiply_fusion.1
  500.7 1.9 broadcast_multiply_fusion
  (436 shorter events, 10.0 us)
Async XLA Ops:
  7.2 31.2 %copy-start = (bf16[45,24,128]{2,1,0:T(8,128)(2,1)S(1)}, bf16[45,24,128]{2,1,0:T(8,128)(2,1)}, u32[]{:S(2)}) copy-start(bf16[45,24,128]{2,1,0:T(8,128)(2,1)} %param.12) | copy-start | bytes 829444
  7.2 491.6 %all-reduce.4.cloned.1.call-start = ((), (), s32[]{:S(2)}) async-start(), calls=%async_computation | async-start | bytes 2097152 | tf_op jit(solution)/shard_map/psum | solution.py:184
  8.2 20.2 %collective-permute-start = (bf16[45,3,128]{2,1,0:T(4,128)(2,1)S(1)}, bf16[45,3,128]{2,1,0:T(4,128)(2,1)S(1)}, u32[]{:S(2)}, u32[]{:S(2)}) collective-permute-start(bf16[45,3,128]{2,1,0:T(4,128)(2,1)S(1)} %get-tuple-element.207), channel_id=1, source_target_pairs={{0,8},{8,16},{16,24},{24,32},{32,40},{40,48},{48,56},{56,64},{64,7... | collective-permute-start | bytes 103688 | tf_op jit(solution)/shard_map/ppermute | solution.py:21
  8.3 20.1 %collective-permute-start.1 = (bf16[45,3,128]{2,1,0:T(4,128)(2,1)S(1)}, bf16[45,3,128]{2,1,0:T(4,128)(2,1)S(1)}, u32[]{:S(2)}, u32[]{:S(2)}) collective-permute-start(bf16[45,3,128]{2,1,0:T(4,128)(2,1)S(1)} %get-tuple-element.208), channel_id=1, source_target_pairs={{8,0},{16,8},{24,16},{32,24},{40,32},{48,40},{56,48},{64,56},{72,6... | collective-permute-start | bytes 103688 | tf_op jit(solution)/shard_map/ppermute | solution.py:22
  17.2 26.3 %copy-start.25 = (f32[128]{0:T(128)}, f32[128]{0:T(128)S(1)}, u32[]{:S(2)}) copy-start(f32[128]{0:T(128)S(1)} %get-tuple-element.298) | copy-start | bytes 1540
  17.2 26.3 %copy-start.27 = (f32[128]{0:T(128)}, f32[128]{0:T(128)S(1)}, u32[]{:S(2)}) copy-start(f32[128]{0:T(128)S(1)} %get-tuple-element.299) | copy-start | bytes 1540
  17.3 26.3 %copy-start.29 = (f32[128]{0:T(128)}, f32[128]{0:T(128)S(1)}, u32[]{:S(2)}) copy-start(f32[128]{0:T(128)S(1)} %get-tuple-element.300) | copy-start | bytes 1540
  17.3 26.3 %copy-start.31 = (f32[128]{0:T(128)}, f32[128]{0:T(128)S(1)}, u32[]{:S(2)}) copy-start(f32[128]{0:T(128)S(1)} %get-tuple-element.301) | copy-start | bytes 1540
  17.3 26.3 %copy-start.33 = (f32[128]{0:T(128)}, f32[128]{0:T(128)S(1)}, u32[]{:S(2)}) copy-start(f32[128]{0:T(128)S(1)} %get-tuple-element.302) | copy-start | bytes 1540
  17.3 26.3 %copy-start.35 = (f32[128]{0:T(128)}, f32[128]{0:T(128)S(1)}, u32[]{:S(2)}) copy-start(f32[128]{0:T(128)S(1)} %get-tuple-element.303) | copy-start | bytes 1540
  17.3 26.3 %copy-start.37 = (f32[128]{0:T(128)}, f32[128]{0:T(128)S(1)}, u32[]{:S(2)}) copy-start(f32[128]{0:T(128)S(1)} %get-tuple-element.304) | copy-start | bytes 1540
  17.3 26.3 %copy-start.39 = (f32[128]{0:T(128)}, f32[128]{0:T(128)S(1)}, u32[]{:S(2)}) copy-start(f32[128]{0:T(128)S(1)} %get-tuple-element.305) | copy-start | bytes 1540
  17.3 26.3 %copy-start.41 = (f32[128]{0:T(128)}, f32[128]{0:T(128)S(1)}, u32[]{:S(2)}) copy-start(f32[128]{0:T(128)S(1)} %get-tuple-element.306) | copy-start | bytes 1540
  17.3 26.3 %copy-start.43 = (f32[128]{0:T(128)}, f32[128]{0:T(128)S(1)}, u32[]{:S(2)}) copy-start(f32[128]{0:T(128)S(1)} %get-tuple-element.307) | copy-start | bytes 1540
  17.3 26.3 %copy-start.45 = (f32[128]{0:T(128)}, f32[128]{0:T(128)S(1)}, u32[]{:S(2)}) copy-start(f32[128]{0:T(128)S(1)} %get-tuple-element.308) | copy-start | bytes 1540
  17.4 26.3 %copy-start.47 = (f32[128]{0:T(128)}, f32[128]{0:T(128)S(1)}, u32[]{:S(2)}) copy-start(f32[128]{0:T(128)S(1)} %get-tuple-element.279) | copy-start | bytes 1540
  17.4 26.3 %copy-start.49 = (f32[128]{0:T(128)}, f32[128]{0:T(128)S(1)}, u32[]{:S(2)}) copy-start(f32[128]{0:T(128)S(1)} %get-tuple-element.280) | copy-start | bytes 1540
  17.4 26.3 %copy-start.51 = (f32[128]{0:T(128)}, f32[128]{0:T(128)S(1)}, u32[]{:S(2)}) copy-start(f32[128]{0:T(128)S(1)} %get-tuple-element.281) | copy-start | bytes 1540
  17.4 26.3 %copy-start.53 = (f32[128]{0:T(128)}, f32[128]{0:T(128)S(1)}, u32[]{:S(2)}) copy-start(f32[128]{0:T(128)S(1)} %get-tuple-element.282) | copy-start | bytes 1540
  17.4 26.3 %copy-start.55 = (f32[128]{0:T(128)}, f32[128]{0:T(128)S(1)}, u32[]{:S(2)}) copy-start(f32[128]{0:T(128)S(1)} %get-tuple-element.283) | copy-start | bytes 1540
  17.4 26.3 %copy-start.57 = (f32[128]{0:T(128)}, f32[128]{0:T(128)S(1)}, u32[]{:S(2)}) copy-start(f32[128]{0:T(128)S(1)} %get-tuple-element.284) | copy-start | bytes 1540
  17.4 26.3 %copy-start.59 = (f32[128]{0:T(128)}, f32[128]{0:T(128)S(1)}, u32[]{:S(2)}) copy-start(f32[128]{0:T(128)S(1)} %get-tuple-element.285) | copy-start | bytes 1540
  17.4 26.3 %copy-start.61 = (f32[128]{0:T(128)}, f32[128]{0:T(128)S(1)}, u32[]{:S(2)}) copy-start(f32[128]{0:T(128)S(1)} %get-tuple-element.286) | copy-start | bytes 1540
  17.4 26.3 %copy-start.63 = (f32[128]{0:T(128)}, f32[128]{0:T(128)S(1)}, u32[]{:S(2)}) copy-start(f32[128]{0:T(128)S(1)} %get-tuple-element.287) | copy-start | bytes 1540
  17.5 26.3 %copy-start.65 = (f32[128]{0:T(128)}, f32[128]{0:T(128)S(1)}, u32[]{:S(2)}) copy-start(f32[128]{0:T(128)S(1)} %get-tuple-element.288) | copy-start | bytes 1540
  17.5 26.3 %copy-start.67 = (f32[128]{0:T(128)}, f32[128]{0:T(128)S(1)}, u32[]{:S(2)}) copy-start(f32[128]{0:T(128)S(1)} %get-tuple-element.289) | copy-start | bytes 1540
  17.5 26.3 %copy-start.69 = (f32[128]{0:T(128)}, f32[128]{0:T(128)S(1)}, u32[]{:S(2)}) copy-start(f32[128]{0:T(128)S(1)} %get-tuple-element.290) | copy-start | bytes 1540
  17.5 26.3 %copy-start.71 = (f32[128]{0:T(128)}, f32[128]{0:T(128)S(1)}, u32[]{:S(2)}) copy-start(f32[128]{0:T(128)S(1)} %get-tuple-element.291) | copy-start | bytes 1540
  17.5 26.3 %copy-start.73 = (f32[128]{0:T(128)}, f32[128]{0:T(128)S(1)}, u32[]{:S(2)}) copy-start(f32[128]{0:T(128)S(1)} %get-tuple-element.292) | copy-start | bytes 1540
  17.5 26.3 %copy-start.75 = (f32[128]{0:T(128)}, f32[128]{0:T(128)S(1)}, u32[]{:S(2)}) copy-start(f32[128]{0:T(128)S(1)} %get-tuple-element.293) | copy-start | bytes 1540
  17.5 26.3 %copy-start.77 = (f32[128]{0:T(128)}, f32[128]{0:T(128)S(1)}, u32[]{:S(2)}) copy-start(f32[128]{0:T(128)S(1)} %get-tuple-element.294) | copy-start | bytes 1540
  17.5 26.3 %copy-start.79 = (f32[128]{0:T(128)}, f32[128]{0:T(128)S(1)}, u32[]{:S(2)}) copy-start(f32[128]{0:T(128)S(1)} %get-tuple-element.295) | copy-start | bytes 1540
  17.5 26.3 %copy-start.81 = (f32[128]{0:T(128)}, f32[128]{0:T(128)S(1)}, u32[]{:S(2)}) copy-start(f32[128]{0:T(128)S(1)} %get-tuple-element.296) | copy-start | bytes 1540
  17.5 26.3 %copy-start.83 = (f32[128]{0:T(128)}, f32[128]{0:T(128)S(1)}, u32[]{:S(2)}) copy-start(f32[128]{0:T(128)S(1)} %get-tuple-element.297) | copy-start | bytes 1540
  18.2 25.7 %copy-start.85 = (f32[128]{0:T(128)}, f32[128]{0:T(128)S(1)}, u32[]{:S(2)}) copy-start(f32[128]{0:T(128)S(1)} %get-tuple-element.260) | copy-start | bytes 1540
  18.2 25.7 %copy-start.87 = (f32[128]{0:T(128)}, f32[128]{0:T(128)S(1)}, u32[]{:S(2)}) copy-start(f32[128]{0:T(128)S(1)} %get-tuple-element.261) | copy-start | bytes 1540
  18.2 25.7 %copy-start.89 = (f32[128]{0:T(128)}, f32[128]{0:T(128)S(1)}, u32[]{:S(2)}) copy-start(f32[128]{0:T(128)S(1)} %get-tuple-element.262) | copy-start | bytes 1540
  18.2 25.7 %copy-start.91 = (f32[128]{0:T(128)}, f32[128]{0:T(128)S(1)}, u32[]{:S(2)}) copy-start(f32[128]{0:T(128)S(1)} %get-tuple-element.263) | copy-start | bytes 1540
  18.2 25.7 %copy-start.93 = (f32[128]{0:T(128)}, f32[128]{0:T(128)S(1)}, u32[]{:S(2)}) copy-start(f32[128]{0:T(128)S(1)} %get-tuple-element.264) | copy-start | bytes 1540
  18.2 25.7 %copy-start.95 = (f32[128]{0:T(128)}, f32[128]{0:T(128)S(1)}, u32[]{:S(2)}) copy-start(f32[128]{0:T(128)S(1)} %get-tuple-element.265) | copy-start | bytes 1540
  18.2 25.7 %copy-start.97 = (f32[128]{0:T(128)}, f32[128]{0:T(128)S(1)}, u32[]{:S(2)}) copy-start(f32[128]{0:T(128)S(1)} %get-tuple-element.266) | copy-start | bytes 1540
  24.9 25.9 %copy-start.20 = (f32[128]{0:T(128)}, f32[128]{0:T(128)S(1)}, u32[]{:S(2)}) copy-start(f32[128]{0:T(128)S(1)} %get-tuple-element.337) | copy-start | bytes 1540
  29.2 5.9 %collective-permute-start.2 = (bf16[3,30,128]{2,1,0:T(8,128)(2,1)S(1)}, bf16[3,30,128]{2,1,0:T(8,128)(2,1)S(1)}, u32[]{:S(2)}, u32[]{:S(2)}) collective-permute-start(bf16[3,30,128]{2,1,0:T(8,128)(2,1)S(1)} %get-tuple-element.198), channel_id=1, source_target_pairs={{0,1},{1,2},{2,3},{3,4},{4,5},{5,6},{6,7},{8,9},{9,10},{10,11},{11... | collective-permute-start | bytes 69128 | tf_op jit(solution)/shard_map/ppermute | solution.py:21
  32.6 5.7 %collective-permute-start.3 = (bf16[3,30,128]{2,1,0:T(8,128)(2,1)S(1)}, bf16[3,30,128]{2,1,0:T(8,128)(2,1)S(1)}, u32[]{:S(2)}, u32[]{:S(2)}) collective-permute-start(bf16[3,30,128]{2,1,0:T(8,128)(2,1)S(1)} %get-tuple-element.199), channel_id=1, source_target_pairs={{1,0},{2,1},{3,2},{4,3},{5,4},{6,5},{7,6},{9,8},{10,9},{11,10},{12... | collective-permute-start | bytes 69128 | tf_op jit(solution)/shard_map/ppermute | solution.py:22
  53.1 7.2 %collective-permute-start.4 = (bf16[45,3,128]{2,1,0:T(4,128)(2,1)S(1)}, bf16[45,3,128]{2,1,0:T(4,128)(2,1)S(1)}, u32[]{:S(2)}, u32[]{:S(2)}) collective-permute-start(bf16[45,3,128]{2,1,0:T(4,128)(2,1)S(1)} %get-tuple-element.205), channel_id=1, source_target_pairs={{0,8},{8,16},{16,24},{24,32},{32,40},{40,48},{48,56},{56,64},{64,7... | collective-permute-start | bytes 103688 | tf_op jit(solution)/shard_map/ppermute | solution.py:21
  53.2 7.1 %collective-permute-start.5 = (bf16[45,3,128]{2,1,0:T(4,128)(2,1)S(1)}, bf16[45,3,128]{2,1,0:T(4,128)(2,1)S(1)}, u32[]{:S(2)}, u32[]{:S(2)}) collective-permute-start(bf16[45,3,128]{2,1,0:T(4,128)(2,1)S(1)} %get-tuple-element.206), channel_id=1, source_target_pairs={{8,0},{16,8},{24,16},{32,24},{40,32},{48,40},{56,48},{64,56},{72,6... | collective-permute-start | bytes 103688 | tf_op jit(solution)/shard_map/ppermute | solution.py:22
  60.3 6.5 %collective-permute-start.6 = (bf16[3,30,128]{2,1,0:T(8,128)(2,1)S(1)}, bf16[3,30,128]{2,1,0:T(8,128)(2,1)S(1)}, u32[]{:S(2)}, u32[]{:S(2)}) collective-permute-start(bf16[3,30,128]{2,1,0:T(8,128)(2,1)S(1)} %get-tuple-element.194), channel_id=1, source_target_pairs={{0,1},{1,2},{2,3},{3,4},{4,5},{5,6},{6,7},{8,9},{9,10},{10,11},{11... | collective-permute-start | bytes 69128 | tf_op jit(solution)/shard_map/ppermute | solution.py:21
  63.4 6.4 %collective-permute-start.7 = (bf16[3,30,128]{2,1,0:T(8,128)(2,1)S(1)}, bf16[3,30,128]{2,1,0:T(8,128)(2,1)S(1)}, u32[]{:S(2)}, u32[]{:S(2)}) collective-permute-start(bf16[3,30,128]{2,1,0:T(8,128)(2,1)S(1)} %get-tuple-element.195), channel_id=1, source_target_pairs={{1,0},{2,1},{3,2},{4,3},{5,4},{6,5},{7,6},{9,8},{10,9},{11,10},{12... | collective-permute-start | bytes 69128 | tf_op jit(solution)/shard_map/ppermute | solution.py:22
  93.0 22.3 %copy-start.24 = (f32[128]{0:T(128)S(1)}, f32[128]{0:T(128)}, u32[]{:S(2)}) copy-start(f32[128]{0:T(128)} %get-tuple-element.319) | copy-start | bytes 1540
  93.0 7.3 %collective-permute-start.8 = (bf16[45,3,128]{2,1,0:T(4,128)(2,1)S(1)}, bf16[45,3,128]{2,1,0:T(4,128)(2,1)S(1)}, u32[]{:S(2)}, u32[]{:S(2)}) collective-permute-start(bf16[45,3,128]{2,1,0:T(4,128)(2,1)S(1)} %get-tuple-element.203), channel_id=1, source_target_pairs={{0,8},{8,16},{16,24},{24,32},{32,40},{40,48},{48,56},{56,64},{64,7... | collective-permute-start | bytes 103688 | tf_op jit(solution)/shard_map/ppermute | solution.py:21
  93.1 7.3 %collective-permute-start.9 = (bf16[45,3,128]{2,1,0:T(4,128)(2,1)S(1)}, bf16[45,3,128]{2,1,0:T(4,128)(2,1)S(1)}, u32[]{:S(2)}, u32[]{:S(2)}) collective-permute-start(bf16[45,3,128]{2,1,0:T(4,128)(2,1)S(1)} %get-tuple-element.204), channel_id=1, source_target_pairs={{8,0},{16,8},{24,16},{32,24},{40,32},{48,40},{56,48},{64,56},{72,6... | collective-permute-start | bytes 103688 | tf_op jit(solution)/shard_map/ppermute | solution.py:22
  100.3 21.6 %copy-start.4 = (bf16[45,24,128]{2,1,0:T(8,128)(2,1)S(1)}, bf16[45,24,128]{2,1,0:T(8,128)(2,1)}, u32[]{:S(2)}) copy-start(bf16[45,24,128]{2,1,0:T(8,128)(2,1)} %param.14) | copy-start | bytes 829444
  100.3 21.6 %copy-start.21 = (f32[128]{0:T(128)S(1)}, f32[128]{0:T(128)}, u32[]{:S(2)}) copy-start(f32[128]{0:T(128)} %copy-done.20) | copy-start | bytes 1540
  100.3 21.6 %copy-start.100 = (f32[128]{0:T(128)S(1)}, f32[128]{0:T(128)}, u32[]{:S(2)}) copy-start(f32[128]{0:T(128)} %copy-done.99) | copy-start | bytes 1540
  100.3 21.6 %copy-start.102 = (f32[128]{0:T(128)S(1)}, f32[128]{0:T(128)}, u32[]{:S(2)}) copy-start(f32[128]{0:T(128)} %copy-done.101) | copy-start | bytes 1540
  100.3 21.6 %copy-start.104 = (f32[128]{0:T(128)S(1)}, f32[128]{0:T(128)}, u32[]{:S(2)}) copy-start(f32[128]{0:T(128)} %copy-done.103) | copy-start | bytes 1540
  100.4 20.3 %collective-permute-start.10 = (bf16[3,30,128]{2,1,0:T(8,128)(2,1)S(1)}, bf16[3,30,128]{2,1,0:T(8,128)(2,1)S(1)}, u32[]{:S(2)}, u32[]{:S(2)}) collective-permute-start(bf16[3,30,128]{2,1,0:T(8,128)(2,1)S(1)} %get-tuple-element.190), channel_id=1, source_target_pairs={{1,0},{2,1},{3,2},{4,3},{5,4},{6,5},{7,6},{9,8},{10,9},{11,10},{12... | collective-permute-start | bytes 69128 | tf_op jit(solution)/shard_map/ppermute | solution.py:22
  102.6 18.2 %collective-permute-start.11 = (bf16[3,30,128]{2,1,0:T(8,128)(2,1)S(1)}, bf16[3,30,128]{2,1,0:T(8,128)(2,1)S(1)}, u32[]{:S(2)}, u32[]{:S(2)}) collective-permute-start(bf16[3,30,128]{2,1,0:T(8,128)(2,1)S(1)} %get-tuple-element.191), channel_id=1, source_target_pairs={{0,1},{1,2},{2,3},{3,4},{4,5},{5,6},{6,7},{8,9},{9,10},{10,11},{11... | collective-permute-start | bytes 69128 | tf_op jit(solution)/shard_map/ppermute | solution.py:21
  140.7 87.8 %copy-start.18 = (bf16[45,3,128]{2,1,0:T(4,128)(2,1)S(1)}, bf16[45,3,128]{2,1,0:T(4,128)(2,1)}, u32[]{:S(2)}) copy-start(bf16[45,3,128]{2,1,0:T(4,128)(2,1)} %get-tuple-element.201) | copy-start | bytes 103684
  140.8 101.8 %copy-start.6 = (f32[1,128,512]{2,1,0:T(8,128)S(1)}, f32[1,128,512]{2,1,0:T(8,128)}, u32[]{:S(2)}) copy-start(f32[1,128,512]{2,1,0:T(8,128)} %convolution_bitcast_fusion.3) | copy-start | bytes 786436
  228.6 2.1 collective-permute-start.13
  229.3 7.4 %collective-permute-start.12 = (bf16[45,3,128]{2,1,0:T(4,128)(2,1)S(1)}, bf16[45,3,128]{2,1,0:T(4,128)(2,1)S(1)}, u32[]{:S(2)}, u32[]{:S(2)}) collective-permute-start(bf16[45,3,128]{2,1,0:T(4,128)(2,1)S(1)} %get-tuple-element.202), channel_id=1, source_target_pairs={{0,8},{8,16},{16,24},{24,32},{32,40},{40,48},{48,56},{56,64},{64,7... | collective-permute-start | bytes 103688 | tf_op jit(solution)/shard_map/ppermute | solution.py:21
  236.7 7.4 %collective-permute-start.14 = (bf16[3,30,128]{2,1,0:T(8,128)(2,1)S(1)}, bf16[3,30,128]{2,1,0:T(8,128)(2,1)S(1)}, u32[]{:S(2)}, u32[]{:S(2)}) collective-permute-start(bf16[3,30,128]{2,1,0:T(8,128)(2,1)S(1)} %get-tuple-element.186), channel_id=1, source_target_pairs={{1,0},{2,1},{3,2},{4,3},{5,4},{6,5},{7,6},{9,8},{10,9},{11,10},{12... | collective-permute-start | bytes 69128 | tf_op jit(solution)/shard_map/ppermute | solution.py:22
  239.3 5.7 %collective-permute-start.15 = (bf16[3,30,128]{2,1,0:T(8,128)(2,1)S(1)}, bf16[3,30,128]{2,1,0:T(8,128)(2,1)S(1)}, u32[]{:S(2)}, u32[]{:S(2)}) collective-permute-start(bf16[3,30,128]{2,1,0:T(8,128)(2,1)S(1)} %get-tuple-element.187), channel_id=1, source_target_pairs={{0,1},{1,2},{2,3},{3,4},{4,5},{5,6},{6,7},{8,9},{9,10},{10,11},{11... | collective-permute-start | bytes 69128 | tf_op jit(solution)/shard_map/ppermute | solution.py:21
  (139 other events, 1425.3 us)
Sparse Core Ops, SparseCore 0:
  244.2 254.5 all-reduce.3
where the time goes:
time: 517 us; the launch traced here: 510 us
  waiting for transfers between devices  262 us (51%)
  blocking collectives  81.3 us (16%)
  starting transfers between devices  52.5 us (10%)
  other arithmetic  52.3 us (10%)
  matrix products  25.1 us (5%)
  local copies, waits for them, and re-layouts  18.7 us (4%)
  between operations  17.3 us (3%)
    psum x1, waiting for transfers between devices, sum_everything(): lax.psum((kernel_part, conv_part, gain_part, shift_part, first_part, firs...  247 us
    psum x1, blocking collectives, sum_everything(): lax.psum((kernel_part, conv_part, gain_part, shift_part, first_part, firs...  81.3 us
    ppermute x8, starting transfers between devices, with_halo(): after = lax.ppermute(first, axis, down)  29.4 us
    ppermute x8, starting transfers between devices, with_halo(): before = lax.ppermute(last, axis, up)  23 us
    dot_general x2, matrix products, block_forward(): jnp.dot(lifted, weight_in, preferred_element_type=jnp.float32) + bias_in  13 us
  transfers between devices with their start and end apart: 17, of which 7 were waited for; matrix products, arithmetic and copies ran while one was open for 5% of the time, Pallas kernels for 0%

commit v1 on v0

--- a/solution.py
+++ b/solution.py
@@ -182,18 +182,21 @@
         scale_part,
     ) = parts
     return lax.psum(
-        (
-            kernel_part,
-            conv_part,
-            gain_part,
-            shift_part,
-            first_part,
-            first_bias,
-            second_part,
-            second_bias,
-            scale_part,
+        lax.psum(
+            (
+                kernel_part,
+                conv_part,
+                gain_part,
+                shift_part,
+                first_part,
+                first_bias,
+                second_part,
+                second_bias,
+                scale_part,
+            ),
+            "lat",
         ),
-        ("lon", "lat"),
+        "lon",
     )
 
 

time: 517 us -> 688 us (1.33)
  waiting for transfers between devices: 262 us -> 350 us
  blocking collectives: 81.3 us -> 162 us
    psum x0 -> x1, waiting for transfers between devices: none -> 269 us  [sum_everything(): lax.psum(lax.psum((kernel_part, conv_part, gain_part, shift_part, first_p...]
    psum x1, waiting for transfers between devices: 247 us -> 69.5 us  [sum_everything(): lax.psum((kernel_part, conv_part, gain_part, shift_part, first_part, firs...]
    psum x0 -> x1, blocking collectives: none -> 129 us  [sum_everything(): lax.psum(lax.psum((kernel_part, conv_part, gain_part, shift_part, first_p...]
    psum x1, blocking collectives: 81.3 us -> 33.2 us  [sum_everything(): lax.psum((kernel_part, conv_part, gain_part, shift_part, first_part, firs...]
  transfers between devices with their start and end apart: 17 -> 18, of which waited for: 7 -> 7; matrix products, arithmetic and copies ran while one was open for 5% -> 4% of each run, Pallas kernels for 0% -> 0%
where the time goes in v1:
time: 688 us; the launch traced here: 679 us
  waiting for transfers between devices  350 us (51%)
  blocking collectives  162 us (24%)
  starting transfers between devices  54.6 us (8%)
  other arithmetic  52.3 us (8%)
  matrix products  24.7 us (4%)
  local copies, waits for them, and re-layouts  18 us (3%)
  between operations  17.4 us (3%)
    psum x1, waiting for transfers between devices, sum_everything(): lax.psum(lax.psum((kernel_part, conv_part, gain_part, shift_part, first_p...  269 us
    psum x1, blocking collectives, sum_everything(): lax.psum(lax.psum((kernel_part, conv_part, gain_part, shift_part, first_p...  129 us
    psum x1, waiting for transfers between devices, sum_everything(): lax.psum((kernel_part, conv_part, gain_part, shift_part, first_part, firs...  69.5 us
    psum x1, blocking collectives, sum_everything(): lax.psum((kernel_part, conv_part, gain_part, shift_part, first_part, firs...  33.2 us
    ppermute x8, starting transfers between devices, with_halo(): after = lax.ppermute(first, axis, down)  30.6 us
    ppermute x8, starting transfers between devices, with_halo(): before = lax.ppermute(last, axis, up)  23.9 us
  transfers between devices with their start and end apart: 18, of which 7 were waited for; matrix products, arithmetic and copies ran while one was open for 4% of the time, Pallas kernels for 0%

profile of v1, /device:TPU:2, one launch (start us, length us, event | category | flops | bytes accessed | tf_op | source)
XLA Modules:
  0.0 678.7 jit_solution(4009976590486737089)
XLA Ops:
  7.2 1.0 fusion.426
  8.3 8.0 %collective-permute-start.1 = (bf16[45,3,128]{2,1,0:T(4,128)(2,1)S(1)}, bf16[45,3,128]{2,1,0:T(4,128)(2,1)S(1)}, u32[]{:S(2)}, u32[]{:S(2)}) collective-permute-start(bf16[45,3,128]{2,1,0:T(4,128)(2,1)S(1)} %get-tuple-element.217), channel_id=1, source_target_pairs={{8,0},{16,8},{24,16},{32,24},{40,32},{48,40},{56,48},{64,56},{72,6... | collective-permute-start | bytes 103688 | tf_op jit(solution)/shard_map/ppermute | solution.py:22
  16.3 0.9 fusion.427
  17.6 0.6 fusion.415
  18.2 1.3 slice_bitcast_fusion.101
  19.5 1.3 fusion.428
  20.9 0.7 convert_element_type.1162
  21.7 0.7 fusion.365
  22.3 1.3 slice_bitcast_fusion.99
  23.6 1.3 slice_bitcast_fusion.98
  24.9 2.5 convert_reduce_fusion.3
  27.3 1.0 constant_dynamic-update-slice_fusion.1
  28.4 0.8 pad_maximum_fusion.25
  29.2 3.4 collective-permute-start.2
  32.6 2.4 collective-permute-start.3
  35.1 3.2 collective-permute-done.3
  38.6 5.0 fusion.421
  44.7 6.0 fusion.4
  50.8 1.0 copy-done.2
  51.8 1.3 fusion.277
  53.2 5.3 collective-permute-start.5
  58.8 1.5 collective-permute-done.4
  60.3 3.1 collective-permute-start.6
  63.4 3.1 collective-permute-start.7
  66.8 3.1 collective-permute-done.7
  70.1 5.0 fusion.419
  75.4 0.8 copy-done.1
  77.2 1.5 add_convert_fusion.2
  78.7 7.0 %fusion.7 = (bf16[1080,512]{1,0:T(8,128)(2,1)}, f32[1080,512]{1,0:T(8,128)S(1)}) fusion(f32[512]{0:T(512)} %bitcast.780, bf16[1080,128]{1,0:T(8,128)(2,1)S(1)} %bitcast.741, bf16[2,128,512]{2,1,0:T(8,128)(2,1)} %param.19), kind=kOutput, calls=%fused_computation.116 | convolution fusion | flops 178053120 | bytes 3727360 | tf_op jit(solution)/shard_map/dot_general | solution.py:60
  85.7 1.9 convert_reduce_fusion
  87.6 1.1 fusion.417
  88.7 1.0 convert_reduce_fusion.2
  89.8 1.6 fusion.201
  91.4 1.6 fusion.174
  93.1 5.3 collective-permute-start.9
  98.5 1.7 fusion.200
  100.4 2.2 collective-permute-start.10
  102.6 12.7 %collective-permute-start.11 = (bf16[3,30,128]{2,1,0:T(8,128)(2,1)S(1)}, bf16[3,30,128]{2,1,0:T(8,128)(2,1)S(1)}, u32[]{:S(2)}, u32[]{:S(2)}) collective-permute-start(bf16[3,30,128]{2,1,0:T(8,128)(2,1)S(1)} %get-tuple-element.200), channel_id=1, source_target_pairs={{0,1},{1,2},{2,3},{3,4},{4,5},{5,6},{6,7},{8,9},{9,10},{10,11},{11... | collective-permute-start | bytes 69128 | tf_op jit(solution)/shard_map/ppermute | solution.py:21
  115.8 4.9 stack.474
  120.8 1.1 pad_maximum_fusion.4
  122.0 6.2 multiply_convert_fusion.1
  128.5 1.9 convert_reduce_fusion.1
  130.3 1.1 convolution_bitcast_fusion.3
  131.4 0.6 fusion.416
  132.6 1.6 fusion.247
  134.2 1.6 fusion.275
  135.8 0.7 fusion.423
  137.0 2.4 multiply_reduce_fusion.1
  140.3 1.1 fusion.274
  141.9 0.7 pad_maximum_fusion.31
  142.7 33.2 %all-reduce.2 = (f32[2,7,7,128]{3,2,1,0:T(8,128)S(1)}, f32[2,128]{1,0:T(2,128)S(1)}, f32[2,128]{1,0:T(2,128)S(1)}, f32[2,128]{1,0:T(2,128)S(1)}, f32[2,512]{1,0:...) all-reduce(f32[2,7,7,128]{3,2,1,0:T(8,128)S(1)} %pad_maximum_fusion, ...), channel_id=1, replica_groups=mesh['lon'=32,'lat'=8] {'lat'}, use_global_device_ids=true, to_apply=%region_106.0 | all-reduce | flops 14848 | bytes 118784 | tf_op jit(solution)/shard_map/psum | solution.py:185
  175.9 128.6 %all-reduce = (f32[2,7,7,128]{3,2,1,0:T(8,128)S(1)}, f32[2,128]{1,0:T(2,128)S(1)}, f32[2,128]{1,0:T(2,128)S(1)}, f32[2,128]{1,0:T(2,128)S(1)}, f32[2,512]{1,0:T(...) all-reduce(f32[2,7,7,128]{3,2,1,0:T(8,128)S(1)} %get-tuple-element., ...), channel_id=1, replica_groups=mesh['lon'=32,'lat'=8] {'lon'}, use_global_device_ids=true, to_apply=%region_107.0 | all-reduce | flops 14848 | bytes 118784 | tf_op jit(solution)/shard_map/psum | solution.py:184
  305.7 0.6 broadcast_multiply_fusion.9
  306.8 0.8 pad_maximum_fusion.1
  307.6 0.8 pad_maximum_fusion
  310.0 3.4 collective-permute-done.12
  313.4 4.2 collective-permute-start.14
  317.6 3.9 collective-permute-start.15
  322.1 0.6 copy.30
  323.5 69.5 %all-reduce.9.cloned.1.call-done = (f32[2,128,512]{2,1,0:T(8,128)}, f32[2,512,128]{2,1,0:T(8,128)}) async-done(((f32[2,128,512]{2,1,0:T(8,128)}, f32[2,512,128]{2,1,0:T(8,128)}), (f32[2,128,512]{2,1,0:T(8,128)}, f32[2,512,128]{2,1,0:T(8,128)})) %all-reduce.9.cloned.1.call-update) | async-done | bytes 1048592 | tf_op jit(solution)/shard_map/psum | solution.py:185
  393.4 5.8 fusion.280
  399.2 268.7 %all-reduce.7.cloned.1.call-done = (f32[2,128,512]{2,1,0:T(8,128)}, f32[2,512,128]{2,1,0:T(8,128)}) async-done(((f32[2,128,512]{2,1,0:T(8,128)}, f32[2,512,128]{2,1,0:T(8,128)}), (f32[2,128,512]{2,1,0:T(8,128)}, f32[2,512,128]{2,1,0:T(8,128)})) %all-reduce.7.cloned.1.call-update) | async-done | bytes 1048592 | tf_op jit(solution)/shard_map/psum | solution.py:184
  667.9 1.9 broadcast_multiply_fusion.1
  669.8 1.9 broadcast_multiply_fusion
  (440 shorter events, 10.3 us)
Async XLA Ops:
  7.2 31.2 %copy-start = (bf16[45,24,128]{2,1,0:T(8,128)(2,1)S(1)}, bf16[45,24,128]{2,1,0:T(8,128)(2,1)}, u32[]{:S(2)}) copy-start(bf16[45,24,128]{2,1,0:T(8,128)(2,1)} %param.12) | copy-start | bytes 829444
  7.2 385.8 %all-reduce.9.cloned.1.call-start = ((), (), s32[]{:S(2)}) async-start(), calls=%async_computation.1 | async-start | bytes 2097152 | tf_op jit(solution)/shard_map/psum | solution.py:185
  8.2 20.2 %collective-permute-start = (bf16[45,3,128]{2,1,0:T(4,128)(2,1)S(1)}, bf16[45,3,128]{2,1,0:T(4,128)(2,1)S(1)}, u32[]{:S(2)}, u32[]{:S(2)}) collective-permute-start(bf16[45,3,128]{2,1,0:T(4,128)(2,1)S(1)} %get-tuple-element.216), channel_id=1, source_target_pairs={{0,8},{8,16},{16,24},{24,32},{32,40},{40,48},{48,56},{56,64},{64,7... | collective-permute-start | bytes 103688 | tf_op jit(solution)/shard_map/ppermute | solution.py:21
  8.3 20.1 %collective-permute-start.1 = (bf16[45,3,128]{2,1,0:T(4,128)(2,1)S(1)}, bf16[45,3,128]{2,1,0:T(4,128)(2,1)S(1)}, u32[]{:S(2)}, u32[]{:S(2)}) collective-permute-start(bf16[45,3,128]{2,1,0:T(4,128)(2,1)S(1)} %get-tuple-element.217), channel_id=1, source_target_pairs={{8,0},{16,8},{24,16},{32,24},{40,32},{48,40},{56,48},{64,56},{72,6... | collective-permute-start | bytes 103688 | tf_op jit(solution)/shard_map/ppermute | solution.py:22
  17.2 26.3 %copy-start.26 = (f32[128]{0:T(128)}, f32[128]{0:T(128)S(1)}, u32[]{:S(2)}) copy-start(f32[128]{0:T(128)S(1)} %get-tuple-element.308) | copy-start | bytes 1540
  17.3 26.3 %copy-start.28 = (f32[128]{0:T(128)}, f32[128]{0:T(128)S(1)}, u32[]{:S(2)}) copy-start(f32[128]{0:T(128)S(1)} %get-tuple-element.309) | copy-start | bytes 1540
  17.3 26.3 %copy-start.30 = (f32[128]{0:T(128)}, f32[128]{0:T(128)S(1)}, u32[]{:S(2)}) copy-start(f32[128]{0:T(128)S(1)} %get-tuple-element.310) | copy-start | bytes 1540
  17.3 26.3 %copy-start.32 = (f32[128]{0:T(128)}, f32[128]{0:T(128)S(1)}, u32[]{:S(2)}) copy-start(f32[128]{0:T(128)S(1)} %get-tuple-element.311) | copy-start | bytes 1540
  17.3 26.3 %copy-start.34 = (f32[128]{0:T(128)}, f32[128]{0:T(128)S(1)}, u32[]{:S(2)}) copy-start(f32[128]{0:T(128)S(1)} %get-tuple-element.312) | copy-start | bytes 1540
  17.3 26.3 %copy-start.36 = (f32[128]{0:T(128)}, f32[128]{0:T(128)S(1)}, u32[]{:S(2)}) copy-start(f32[128]{0:T(128)S(1)} %get-tuple-element.313) | copy-start | bytes 1540
  17.3 26.3 %copy-start.38 = (f32[128]{0:T(128)}, f32[128]{0:T(128)S(1)}, u32[]{:S(2)}) copy-start(f32[128]{0:T(128)S(1)} %get-tuple-element.314) | copy-start | bytes 1540
  29.2 5.9 collective-permute-start.2
  32.6 5.7 collective-permute-start.3
  53.1 7.2 %collective-permute-start.4 = (bf16[45,3,128]{2,1,0:T(4,128)(2,1)S(1)}, bf16[45,3,128]{2,1,0:T(4,128)(2,1)S(1)}, u32[]{:S(2)}, u32[]{:S(2)}) collective-permute-start(bf16[45,3,128]{2,1,0:T(4,128)(2,1)S(1)} %get-tuple-element.214), channel_id=1, source_target_pairs={{0,8},{8,16},{16,24},{24,32},{32,40},{40,48},{48,56},{56,64},{64,7... | collective-permute-start | bytes 103688 | tf_op jit(solution)/shard_map/ppermute | solution.py:21
  53.2 7.1 %collective-permute-start.5 = (bf16[45,3,128]{2,1,0:T(4,128)(2,1)S(1)}, bf16[45,3,128]{2,1,0:T(4,128)(2,1)S(1)}, u32[]{:S(2)}, u32[]{:S(2)}) collective-permute-start(bf16[45,3,128]{2,1,0:T(4,128)(2,1)S(1)} %get-tuple-element.215), channel_id=1, source_target_pairs={{8,0},{16,8},{24,16},{32,24},{40,32},{48,40},{56,48},{64,56},{72,6... | collective-permute-start | bytes 103688 | tf_op jit(solution)/shard_map/ppermute | solution.py:22
  60.3 6.5 collective-permute-start.6
  63.4 6.4 collective-permute-start.7
  93.0 7.3 %collective-permute-start.8 = (bf16[45,3,128]{2,1,0:T(4,128)(2,1)S(1)}, bf16[45,3,128]{2,1,0:T(4,128)(2,1)S(1)}, u32[]{:S(2)}, u32[]{:S(2)}) collective-permute-start(bf16[45,3,128]{2,1,0:T(4,128)(2,1)S(1)} %get-tuple-element.212), channel_id=1, source_target_pairs={{0,8},{8,16},{16,24},{24,32},{32,40},{40,48},{48,56},{56,64},{64,7... | collective-permute-start | bytes 103688 | tf_op jit(solution)/shard_map/ppermute | solution.py:21
  93.1 7.2 %collective-permute-start.9 = (bf16[45,3,128]{2,1,0:T(4,128)(2,1)S(1)}, bf16[45,3,128]{2,1,0:T(4,128)(2,1)S(1)}, u32[]{:S(2)}, u32[]{:S(2)}) collective-permute-start(bf16[45,3,128]{2,1,0:T(4,128)(2,1)S(1)} %get-tuple-element.213), channel_id=1, source_target_pairs={{8,0},{16,8},{24,16},{32,24},{40,32},{48,40},{56,48},{64,56},{72,6... | collective-permute-start | bytes 103688 | tf_op jit(solution)/shard_map/ppermute | solution.py:22
  100.4 20.3 %collective-permute-start.10 = (bf16[3,30,128]{2,1,0:T(8,128)(2,1)S(1)}, bf16[3,30,128]{2,1,0:T(8,128)(2,1)S(1)}, u32[]{:S(2)}, u32[]{:S(2)}) collective-permute-start(bf16[3,30,128]{2,1,0:T(8,128)(2,1)S(1)} %get-tuple-element.199), channel_id=1, source_target_pairs={{1,0},{2,1},{3,2},{4,3},{5,4},{6,5},{7,6},{9,8},{10,9},{11,10},{12... | collective-permute-start | bytes 69128 | tf_op jit(solution)/shard_map/ppermute | solution.py:22
  102.6 18.2 %collective-permute-start.11 = (bf16[3,30,128]{2,1,0:T(8,128)(2,1)S(1)}, bf16[3,30,128]{2,1,0:T(8,128)(2,1)S(1)}, u32[]{:S(2)}, u32[]{:S(2)}) collective-permute-start(bf16[3,30,128]{2,1,0:T(8,128)(2,1)S(1)} %get-tuple-element.200), channel_id=1, source_target_pairs={{0,1},{1,2},{2,3},{3,4},{4,5},{5,6},{6,7},{8,9},{9,10},{10,11},{11... | collective-permute-start | bytes 69128 | tf_op jit(solution)/shard_map/ppermute | solution.py:21
  140.3 167.3 %copy-start.6 = (f32[1,128,512]{2,1,0:T(8,128)S(1)}, f32[1,128,512]{2,1,0:T(8,128)}, u32[]{:S(2)}) copy-start(f32[1,128,512]{2,1,0:T(8,128)} %convolution_bitcast_fusion.3) | copy-start | bytes 786436
  306.3 3.7 collective-permute-start.13
  306.3 7.1 %collective-permute-start.12 = (bf16[45,3,128]{2,1,0:T(4,128)(2,1)S(1)}, bf16[45,3,128]{2,1,0:T(4,128)(2,1)S(1)}, u32[]{:S(2)}, u32[]{:S(2)}) collective-permute-start(bf16[45,3,128]{2,1,0:T(4,128)(2,1)S(1)} %get-tuple-element.211), channel_id=1, source_target_pairs={{0,8},{8,16},{16,24},{24,32},{32,40},{40,48},{48,56},{56,64},{64,7... | collective-permute-start | bytes 103688 | tf_op jit(solution)/shard_map/ppermute | solution.py:21
  308.4 84.6 %copy-start.25 = (f32[128]{0:T(128)S(1)}, f32[128]{0:T(128)}, u32[]{:S(2)}) copy-start(f32[128]{0:T(128)} %copy-done.24) | copy-start | bytes 1540
  308.4 84.6 %copy-start.27 = (f32[128]{0:T(128)S(1)}, f32[128]{0:T(128)}, u32[]{:S(2)}) copy-start(f32[128]{0:T(128)} %copy-done.26) | copy-start | bytes 1540
  308.4 84.6 %copy-start.29 = (f32[128]{0:T(128)S(1)}, f32[128]{0:T(128)}, u32[]{:S(2)}) copy-start(f32[128]{0:T(128)} %copy-done.28) | copy-start | bytes 1540
  308.4 84.6 %copy-start.31 = (f32[128]{0:T(128)S(1)}, f32[128]{0:T(128)}, u32[]{:S(2)}) copy-start(f32[128]{0:T(128)} %copy-done.30) | copy-start | bytes 1540
  308.5 84.6 %copy-start.33 = (f32[128]{0:T(128)S(1)}, f32[128]{0:T(128)}, u32[]{:S(2)}) copy-start(f32[128]{0:T(128)} %copy-done.32) | copy-start | bytes 1540
  308.5 84.6 %copy-start.35 = (f32[128]{0:T(128)S(1)}, f32[128]{0:T(128)}, u32[]{:S(2)}) copy-start(f32[128]{0:T(128)} %copy-done.34) | copy-start | bytes 1540
  308.5 84.6 %copy-start.37 = (f32[128]{0:T(128)S(1)}, f32[128]{0:T(128)}, u32[]{:S(2)}) copy-start(f32[128]{0:T(128)} %copy-done.36) | copy-start | bytes 1540
  308.5 84.6 %copy-start.39 = (f32[128]{0:T(128)S(1)}, f32[128]{0:T(128)}, u32[]{:S(2)}) copy-start(f32[128]{0:T(128)} %copy-done.38) | copy-start | bytes 1540
  308.5 84.6 %copy-start.41 = (f32[128]{0:T(128)S(1)}, f32[128]{0:T(128)}, u32[]{:S(2)}) copy-start(f32[128]{0:T(128)} %copy-done.40) | copy-start | bytes 1540
  308.5 84.6 %copy-start.43 = (f32[128]{0:T(128)S(1)}, f32[128]{0:T(128)}, u32[]{:S(2)}) copy-start(f32[128]{0:T(128)} %copy-done.42) | copy-start | bytes 1540
  308.5 84.6 %copy-start.45 = (f32[128]{0:T(128)S(1)}, f32[128]{0:T(128)}, u32[]{:S(2)}) copy-start(f32[128]{0:T(128)} %copy-done.44) | copy-start | bytes 1540
  308.5 84.6 %copy-start.47 = (f32[128]{0:T(128)S(1)}, f32[128]{0:T(128)}, u32[]{:S(2)}) copy-start(f32[128]{0:T(128)} %copy-done.46) | copy-start | bytes 1540
  308.5 84.6 %copy-start.49 = (f32[128]{0:T(128)S(1)}, f32[128]{0:T(128)}, u32[]{:S(2)}) copy-start(f32[128]{0:T(128)} %copy-done.48) | copy-start | bytes 1540
  308.5 84.6 %copy-start.51 = (f32[128]{0:T(128)S(1)}, f32[128]{0:T(128)}, u32[]{:S(2)}) copy-start(f32[128]{0:T(128)} %copy-done.50) | copy-start | bytes 1540
  308.6 84.6 %copy-start.53 = (f32[128]{0:T(128)S(1)}, f32[128]{0:T(128)}, u32[]{:S(2)}) copy-start(f32[128]{0:T(128)} %copy-done.52) | copy-start | bytes 1540
  308.6 84.6 %copy-start.55 = (f32[128]{0:T(128)S(1)}, f32[128]{0:T(128)}, u32[]{:S(2)}) copy-start(f32[128]{0:T(128)} %copy-done.54) | copy-start | bytes 1540
  308.6 84.6 %copy-start.57 = (f32[128]{0:T(128)S(1)}, f32[128]{0:T(128)}, u32[]{:S(2)}) copy-start(f32[128]{0:T(128)} %copy-done.56) | copy-start | bytes 1540
  308.6 84.6 %copy-start.59 = (f32[128]{0:T(128)S(1)}, f32[128]{0:T(128)}, u32[]{:S(2)}) copy-start(f32[128]{0:T(128)} %copy-done.58) | copy-start | bytes 1540
  308.6 84.6 %copy-start.61 = (f32[128]{0:T(128)S(1)}, f32[128]{0:T(128)}, u32[]{:S(2)}) copy-start(f32[128]{0:T(128)} %copy-done.60) | copy-start | bytes 1540
  308.6 84.6 %copy-start.63 = (f32[128]{0:T(128)S(1)}, f32[128]{0:T(128)}, u32[]{:S(2)}) copy-start(f32[128]{0:T(128)} %copy-done.62) | copy-start | bytes 1540
  308.6 84.6 %copy-start.65 = (f32[128]{0:T(128)S(1)}, f32[128]{0:T(128)}, u32[]{:S(2)}) copy-start(f32[128]{0:T(128)} %copy-done.64) | copy-start | bytes 1540
  308.6 84.6 %copy-start.67 = (f32[128]{0:T(128)S(1)}, f32[128]{0:T(128)}, u32[]{:S(2)}) copy-start(f32[128]{0:T(128)} %copy-done.66) | copy-start | bytes 1540
  308.6 84.6 %copy-start.69 = (f32[128]{0:T(128)S(1)}, f32[128]{0:T(128)}, u32[]{:S(2)}) copy-start(f32[128]{0:T(128)} %copy-done.68) | copy-start | bytes 1540
  308.6 84.6 %copy-start.71 = (f32[128]{0:T(128)S(1)}, f32[128]{0:T(128)}, u32[]{:S(2)}) copy-start(f32[128]{0:T(128)} %copy-done.70) | copy-start | bytes 1540
  308.7 84.6 %copy-start.73 = (f32[128]{0:T(128)S(1)}, f32[128]{0:T(128)}, u32[]{:S(2)}) copy-start(f32[128]{0:T(128)} %copy-done.72) | copy-start | bytes 1540
  308.7 84.6 %copy-start.75 = (f32[128]{0:T(128)S(1)}, f32[128]{0:T(128)}, u32[]{:S(2)}) copy-start(f32[128]{0:T(128)} %copy-done.74) | copy-start | bytes 1540
  308.7 84.6 %copy-start.77 = (f32[128]{0:T(128)S(1)}, f32[128]{0:T(128)}, u32[]{:S(2)}) copy-start(f32[128]{0:T(128)} %copy-done.76) | copy-start | bytes 1540
  308.7 84.6 %copy-start.79 = (f32[128]{0:T(128)S(1)}, f32[128]{0:T(128)}, u32[]{:S(2)}) copy-start(f32[128]{0:T(128)} %copy-done.78) | copy-start | bytes 1540
  308.7 84.6 %copy-start.81 = (f32[128]{0:T(128)S(1)}, f32[128]{0:T(128)}, u32[]{:S(2)}) copy-start(f32[128]{0:T(128)} %copy-done.80) | copy-start | bytes 1540
  308.7 84.6 %copy-start.83 = (f32[128]{0:T(128)S(1)}, f32[128]{0:T(128)}, u32[]{:S(2)}) copy-start(f32[128]{0:T(128)} %copy-done.82) | copy-start | bytes 1540
  308.7 84.6 %copy-start.85 = (f32[128]{0:T(128)S(1)}, f32[128]{0:T(128)}, u32[]{:S(2)}) copy-start(f32[128]{0:T(128)} %copy-done.84) | copy-start | bytes 1540
  308.7 84.6 %copy-start.87 = (f32[128]{0:T(128)S(1)}, f32[128]{0:T(128)}, u32[]{:S(2)}) copy-start(f32[128]{0:T(128)} %copy-done.86) | copy-start | bytes 1540
  308.7 84.6 %copy-start.89 = (f32[128]{0:T(128)S(1)}, f32[128]{0:T(128)}, u32[]{:S(2)}) copy-start(f32[128]{0:T(128)} %copy-done.88) | copy-start | bytes 1540
  308.7 84.6 %copy-start.91 = (f32[128]{0:T(128)S(1)}, f32[128]{0:T(128)}, u32[]{:S(2)}) copy-start(f32[128]{0:T(128)} %copy-done.90) | copy-start | bytes 1540
  308.8 84.6 %copy-start.93 = (f32[128]{0:T(128)S(1)}, f32[128]{0:T(128)}, u32[]{:S(2)}) copy-start(f32[128]{0:T(128)} %copy-done.92) | copy-start | bytes 1540
  308.8 84.6 %copy-start.95 = (f32[128]{0:T(128)S(1)}, f32[128]{0:T(128)}, u32[]{:S(2)}) copy-start(f32[128]{0:T(128)} %copy-done.94) | copy-start | bytes 1540
  308.8 84.6 %copy-start.97 = (f32[128]{0:T(128)S(1)}, f32[128]{0:T(128)}, u32[]{:S(2)}) copy-start(f32[128]{0:T(128)} %copy-done.96) | copy-start | bytes 1540
  308.8 359.1 %all-reduce.7.cloned.1.call-start = ((), (), s32[]{:S(2)}) async-start(), calls=%async_computation | async-start | bytes 2097152 | tf_op jit(solution)/shard_map/psum | solution.py:184
  313.4 9.4 %collective-permute-start.14 = (bf16[3,30,128]{2,1,0:T(8,128)(2,1)S(1)}, bf16[3,30,128]{2,1,0:T(8,128)(2,1)S(1)}, u32[]{:S(2)}, u32[]{:S(2)}) collective-permute-start(bf16[3,30,128]{2,1,0:T(8,128)(2,1)S(1)} %get-tuple-element.195), channel_id=1, source_target_pairs={{1,0},{2,1},{3,2},{4,3},{5,4},{6,5},{7,6},{9,8},{10,9},{11,10},{12... | collective-permute-start | bytes 69128 | tf_op jit(solution)/shard_map/ppermute | solution.py:22
  317.6 5.7 collective-permute-start.15
  (140 other events, 1758.6 us)
Sparse Core Ops, SparseCore 0:
  308.9 84.0 all-reduce.8
  395.6 272.2 all-reduce.6
